TPU v7x, 512 devices: a whole 4x8x8 slice. The times are simulated.
512 devices in a mesh: head: 8 (over z), tok: 64 (over x, y, core).
Axes of the slice: x: 4, y: 8, z: 8, core: 2. Of those that a mesh axis runs over, the one named last changes fastest.
Arguments:
- patches: bfloat16 [32768, 1280], P('tok')
- row_table: bfloat16 [64, 1280], replicated, may hold values from -0.59765625 to 0.59765625
- col_table: bfloat16 [64, 1280], replicated, may hold values from -0.59765625 to 0.59765625
- qkv_weight: bfloat16 [3, 1280, 1280], P(None, 'head'), may hold values from -0.15625 to 0.15625
- out_weight: bfloat16 [1280, 1280], P('head'), may hold values from -0.15625 to 0.15625
- merge_weight: bfloat16 [1280, 5120], P('head'), may hold values from -0.078125 to 0.078125
- segment_ids: int32 [32768], P('tok'), may hold values from 0 to 63, as said below
- image_grids: int32 [64, 2], replicated, may hold values from 2 to 62, as said below
- image_offsets: int32 [64], replicated, may hold values from 0 to 32736, as said below
- owners: int32 [64], replicated, may hold values from 0 to 63, each once
Outputs:
- delivered: bfloat16 [15872, 1280], P('tok', 'head')
Inputs may be any that keep to these rules, and one draw needn't show every extreme that they name: `segment_ids`: tokens of each image are consecutive and images follow in order; the pair p of token blocks (tokens 2 * p * 512 to 2 * (p + 1) * 512 - 1) holds exactly images 2 * p and 2 * p + 1, with no padding. `image_grids`: heights are even, widths are 16, and height times width is the image's token count. Within an image each 2x2 window of patches is four consecutive tokens (top left, top right, bottom left, bottom right), windows in row-major order. The longest image has exactly 992 tokens. `image_offsets`: the first token of each image, consistent with segment_ids. `owners`: every device index along tok owns exactly one image.
All inputs are finite; a program needn't handle non-finite values.
Results may differ from a plain program's by a relative error of at most 0.019.
Values may be sent and summed in bfloat16 or wider, within the bound.
No kernel may reach another device: no remote copies, remote signals or barrier semaphores. Data moves between devices by JAX's collectives and lax.ppermute only.
A program may use at most 64 MiB of HBM per device.

v0:
```python
import math
import jax
import jax.numpy as jnp
from jax import lax
from jax.sharding import PartitionSpec as P

HEAD_DIM = 80
CAP = 248


def partner(x, axis, apart):
    return lax.ppermute(x, axis, [(i, i ^ 1 << apart) for i in range(lax.axis_size(axis))])


def layer_norm(values):
    centered = values - jnp.mean(values, axis=-1, keepdims=True)
    variance = jnp.mean(centered * centered, axis=-1, keepdims=True)
    return centered * lax.rsqrt(variance + 1e-06)


def grid_place(token_pos, start_tok, width_now):
    local_pos = token_pos - start_tok
    window = local_pos // 4
    quarter = local_pos % 4
    half_width = jnp.maximum(width_now // 2, 1)
    row_index = 2 * (window // half_width) + quarter // 2
    col_index = 2 * (window % half_width) + quarter % 2
    return (row_index, col_index)


def dot_last(left, right):
    return lax.dot_general(
        left, right, (((1,), (1,)), ((), ())), preferred_element_type=jnp.float32
    )


def on_device(
    patches,
    row_table,
    col_table,
    qkv_weight,
    out_weight,
    merge_weight,
    segment_ids,
    image_grids,
    image_offsets,
    owners,
):
    full_weight = lax.all_gather(out_weight, "head", axis=0, tiled=True)
    block_rows = patches.shape[0]
    width_here = qkv_weight.shape[1]
    heads_here = width_here // HEAD_DIM
    image_count = owners.shape[0]
    image_ids = jnp.arange(image_count, dtype=jnp.int32)
    token_pos = lax.axis_index("tok") * block_rows + jnp.arange(block_rows, dtype=jnp.int32)
    member = segment_ids[:, None] == image_ids[None, :]
    start_tok = jnp.sum(jnp.where(member, image_offsets[None, :], 0), axis=1)
    width_now = jnp.sum(jnp.where(member, image_grids[None, :, 1], 0), axis=1)
    row_index, col_index = grid_place(token_pos, start_tok, width_now)
    side_ids = jnp.arange(row_table.shape[0], dtype=jnp.int32)
    row_onehot = (row_index[:, None] == side_ids[None, :]).astype(jnp.bfloat16)
    col_onehot = (col_index[:, None] == side_ids[None, :]).astype(jnp.bfloat16)
    resid = (
        patches.astype(jnp.float32)
        + jnp.dot(row_onehot, row_table, preferred_element_type=jnp.float32)
        + jnp.dot(col_onehot, col_table, preferred_element_type=jnp.float32)
    )
    normed = layer_norm(resid).astype(jnp.bfloat16)
    query_rows = dot_last(normed, qkv_weight[0]).astype(jnp.bfloat16)
    key_rows = dot_last(normed, qkv_weight[1]).astype(jnp.bfloat16)
    value_rows = dot_last(normed, qkv_weight[2]).astype(jnp.bfloat16)
    seg_wire = segment_ids.astype(jnp.bfloat16)
    far_keys, far_values, far_seg = partner((key_rows, value_rows, seg_wire), "tok", 0)
    query_heads = query_rows.reshape(block_rows, heads_here, HEAD_DIM)
    key_heads = jnp.concatenate([key_rows, far_keys], axis=0).reshape(
        2 * block_rows, heads_here, HEAD_DIM
    )
    value_heads = jnp.concatenate([value_rows, far_values], axis=0).reshape(
        2 * block_rows, heads_here, HEAD_DIM
    )
    query_seg = seg_wire.astype(jnp.float32)
    key_seg = jnp.concatenate([seg_wire, far_seg], axis=0).astype(jnp.float32)
    scores = jnp.einsum(
        "qhd,khd->hqk", query_heads, key_heads, preferred_element_type=jnp.float32
    ) * (1.0 / math.sqrt(HEAD_DIM))
    same_image = query_seg[:, None] == key_seg[None, :]
    raw_weights = jnp.where(same_image[None], jnp.exp(scores), 0.0)
    weight_sum = jnp.sum(raw_weights, axis=-1, keepdims=True)
    attn_probs = (raw_weights / weight_sum).astype(jnp.bfloat16)
    mixed = jnp.einsum("hqk,khd->qhd", attn_probs, value_heads, preferred_element_type=jnp.float32)
    attended = mixed.reshape(block_rows, width_here).astype(jnp.bfloat16)
    group = lax.axis_size("head")
    sent = jnp.broadcast_to(attended[None], (group,) + attended.shape)
    gathered = lax.all_to_all(sent, "head", 0, 0, tiled=True)
    head_total = jnp.einsum(
        "ztf,zfd->td",
        gathered,
        full_weight.reshape(group, width_here, -1),
        preferred_element_type=jnp.float32,
    )
    normed_two = layer_norm(resid + head_total).astype(jnp.bfloat16)
    merged = normed_two.reshape(block_rows // 4, 4 * normed_two.shape[1])
    projected = dot_last(merged, merge_weight).astype(jnp.bfloat16)
    places = lax.axis_size("tok")
    rows_here = projected.shape[0]
    share = rows_here // places
    spread = lax.all_to_all(projected.reshape(places, share, width_here), "tok", 0, 0, tiled=True)
    pair_ids = jnp.arange(places // 2, dtype=jnp.int32)
    place_ids = jnp.arange(places, dtype=jnp.int32)
    wanted = (owners.reshape(-1, 2)[None, :, :] == place_ids[:, None, None]).any(axis=2)
    pieces = jnp.dot(
        wanted.astype(jnp.bfloat16),
        spread.reshape(places // 2, 2 * share * width_here),
        preferred_element_type=jnp.float32,
    ).astype(jnp.bfloat16)
    pair_rows = lax.all_to_all(
        pieces.reshape(places, 2 * share, width_here), "tok", 0, 0, tiled=True
    ).reshape(2 * rows_here, width_here)
    owner_mask = owners == lax.axis_index("tok")
    image_id = jnp.sum(jnp.where(owner_mask, image_ids, 0))
    first_row = (
        jnp.sum(jnp.where(owner_mask, image_offsets, 0)) // 4 - image_id // 2 * 2 * rows_here
    )
    merged_count = jnp.sum(jnp.where(owner_mask, image_grids[:, 0] * image_grids[:, 1], 0)) // 4
    slot_ids = jnp.arange(CAP, dtype=jnp.int32)
    got_ids = jnp.arange(2 * rows_here, dtype=jnp.int32)
    row_of = got_ids // share % 2 * rows_here + got_ids // (2 * share) * share + got_ids % share
    slot_of = row_of - first_row
    selector = (slot_of[None, :] == slot_ids[:, None]) & (slot_ids < merged_count)[:, None]
    owner_rows = jnp.dot(
        selector.astype(jnp.bfloat16), pair_rows, preferred_element_type=jnp.float32
    )
    return owner_rows.astype(jnp.bfloat16)


def solution(mesh):
    placed = (
        P("tok", None),
        P(),
        P(),
        P(None, "head", None),
        P("head", None),
        P("head", None),
        P("tok"),
        P(),
        P(),
        P(),
    )
    return jax.shard_map(
        on_device, mesh=mesh, in_specs=placed, out_specs=P("tok", "head"), check_vma=False
    )
```

profile of v0, /device:TPU:1, one launch (start us, length us, event | category | flops | bytes accessed | tf_op | source)
XLA Modules:
  0.0 146.8 jit_solution(14957617930545872145)
XLA Ops:
  6.5 0.0 copy-start
  6.5 0.0 copy-start.2
  6.5 0.0 all-gather.2.cloned.1.call-start
  6.5 0.7 all-gather.2.cloned.1.call-update
  7.3 0.7 slice_bitcast_fusion
  7.9 0.8 select_reduce_fusion
  8.7 0.1 fusion.22
  8.9 2.0 %convolution_add_fusion.1 = f32[512,1280]{1,0:T(8,128)S(1)} fusion(bf16[64,1280]{1,0:T(8,128)(2,1)} %param.11, bf16[512,1280]{1,0:T(8,128)(2,1)} %param.10, s32[512]{0:T(512)S(1)} %get-tuple-element.13), kind=kOutput, calls=%fused_computation.3 | convolution fusion | flops 85229568 | bytes 4098048 | tf_op jit(solution)/shard_map/dot_general | solution.py:65
  10.9 0.0 copy-done.2
  10.9 0.6 fusion.41
  11.5 0.0 copy-start.1
  11.5 0.4 multiply_reduce_fusion.1
  11.9 0.0 copy-start.7
  11.9 0.0 copy-start.3
  12.0 0.3 multiply_convert_fusion.1
  12.3 0.8 copy-done.1
  13.0 0.7 copy-done.7
  13.7 0.6 convolution_convert_fusion
  14.3 8.8 %collective-permute-start.2 = (bf16[512,160]{0,1:T(8,128)(2,1)S(1)}, bf16[512,160]{0,1:T(8,128)(2,1)S(1)}, u32[]{:S(2)}, u32[]{:S(2)}) collective-permute-start(bf16[512,160]{0,1:T(8,128)(2,1)S(1)} %convolution_convert_fusion), channel_id=1, source_target_pairs={{0,1},{1,0},{2,3},{3,2},{4,5},{5,4},{6,7},{7,6},{8,9},{9,8},{10,11... | collective-permute-start | bytes 491528 | tf_op jit(solution)/shard_map/ppermute | solution.py:12
  23.1 0.0 copy-done.3
  23.1 1.9 %collective-permute-start.1 = (bf16[512]{0:T(512)(128)(2,1)S(1)}, bf16[512]{0:T(512)(128)(2,1)S(1)}, u32[]{:S(2)}, u32[]{:S(2)}) collective-permute-start(bf16[512]{0:T(512)(128)(2,1)S(1)} %get-tuple-element.11), channel_id=1, source_target_pairs={{0,1},{1,0},{2,3},{3,2},{4,5},{5,4},{6,7},{7,6},{8,9},{9,8},{10,11... | collective-permute-start | bytes 3080 | tf_op jit(solution)/shard_map/ppermute | solution.py:12
  25.0 0.6 convolution_convert_fusion.2
  25.6 2.4 %collective-permute-start = (bf16[512,160]{0,1:T(8,128)(2,1)S(1)}, bf16[512,160]{0,1:T(8,128)(2,1)S(1)}, u32[]{:S(2)}, u32[]{:S(2)}) collective-permute-start(bf16[512,160]{0,1:T(8,128)(2,1)S(1)} %convolution_convert_fusion.2), channel_id=1, source_target_pairs={{0,1},{1,0},{2,3},{3,2},{4,5},{5,4},{6,7},{7,6},{8,9},{9,8},{10,11... | collective-permute-start | bytes 491528 | tf_op jit(solution)/shard_map/ppermute | solution.py:12
  28.0 0.6 convolution_convert_fusion.1
  28.6 0.0 collective-permute-done.1
  28.6 0.4 broadcast_compare_fusion
  29.0 0.0 collective-permute-done.2
  29.1 0.0 collective-permute-done
  29.1 1.5 %fusion = (f32[2,512]{1,0:T(2,128)S(1)}, f32[2,512,1024]{2,1,0:T(8,128)S(1)}) fusion(pred[512,1024]{1,0:T(8,128)(4,1)S(1)} %broadcast_compare_fusion, bf16[512,2,80]{0,2,1:T(8,128)(2,1)S(1)} %bitcast.49, bf16[1024,2,80]{0,2,1:T(8,128)(2,1)S(1)} %bitcast.46), kind=kOutput, calls=%fused_computation.4 | convolution fusion | flops 170916864 | bytes 5214208 | tf_op jit(solution)/shard_map/qhd,khd->hqk/dot_general | solution.py:83
  30.6 1.4 fusion.3
  31.9 0.0 copy-start.5
  32.0 0.0 copy-start.4
  32.0 0.0 copy-start.6
  32.0 1.2 broadcast_in_dim.69
  33.2 4.7 %all-to-all-start = ((bf16[8,512,160]{1,2,0:T(8,128)(2,1)}), bf16[8,512,160]{1,2,0:T(8,128)(2,1)S(1)}, u32[]{:S(2)}, u32[]{:S(2)}) async-start(bf16[8,512,160]{1,2,0:T(8,128)(2,1)} %broadcast_in_dim.69), calls=%async_computation | async-start | bytes 2621440 | tf_op jit(solution)/shard_map/all_to_all | solution.py:94
  37.8 0.0 copy-done.5
  37.8 0.1 eq.109
  37.9 0.0 copy-done.4
  38.0 0.0 copy-done.6
  38.0 0.7 fusion.37
  40.0 0.1 copy.12
  41.4 44.9 %all-to-all-done = bf16[8,512,160]{1,2,0:T(8,128)(2,1)S(1)} async-done(((bf16[8,512,160]{1,2,0:T(8,128)(2,1)}), bf16[8,512,160]{1,2,0:T(8,128)(2,1)S(1)}, u32[]{:S(2)}, u32[]{:S(2)}) %all-to-all-start) | async-done | bytes 1310752 | tf_op jit(solution)/shard_map/all_to_all | solution.py:94
  86.3 6.4 %all-gather.2.cloned.1.call-done = bf16[1280,1280]{1,0:T(8,128)(2,1)} async-done(((bf16[160,1280]{1,0:T(8,128)(2,1)}), bf16[1280,1280]{1,0:T(8,128)(2,1)}) %all-gather.2.cloned.1.call-update) | async-done | bytes 3276816 | tf_op jit(solution)/shard_map/all_gather | solution.py:49
  92.7 4.8 %fusion.42 = (f32[512]{0:T(512)S(1)}, f32[512,1280]{1,0:T(8,128)S(1)}) fusion(f32[512,1280]{1,0:T(8,128)} %copy-done.1, bf16[8,512,160]{1,2,0:T(8,128)(2,1)S(1)} %all-to-all-done, bf16[8,160,1280]{2,1,0:T(8,128)(2,1)} %bitcast.45), kind=kOutput, calls=%fused_computation.113 | convolution fusion | flops 1679031808 | bytes 9832448 | tf_op jit(solution)/shard_map/ztf,zfd->td/dot_general | solution.py:95
  97.5 0.4 multiply_reduce_fusion
  98.0 0.3 multiply_convert_fusion
  98.3 1.7 %reshape.260 = bf16[128,5120]{1,0:T(8,128)(2,1)} reshape(bf16[512,1280]{1,0:T(8,128)(2,1)S(1)} %multiply_convert_fusion) | data formatting | bytes 2621440 | tf_op jit(solution)/shard_map/reshape | solution.py:102
  100.0 0.0 copy-done
  100.0 1.9 %convolution_convert_fusion.5 = bf16[128,160]{0,1:T(8,128)(2,1)S(1)} fusion(bf16[128,5120]{1,0:T(8,128)(2,1)} %reshape.260, bf16[160,5120]{1,0:T(8,128)(2,1)S(1)} %copy-done), kind=kOutput, calls=%fused_computation.18 | convolution fusion | flops 209735680 | bytes 2990080 | tf_op jit(solution)/shard_map/dot_general | solution.py:32
  101.9 0.1 copy.13
  102.0 0.7 reshape.261
  102.7 10.4 %all-to-all-start.1 = ((bf16[64,2,160]{2,1,0:T(2,128)(2,1)}), bf16[64,2,160]{2,1,0:T(2,128)(2,1)S(1)}, u32[]{:S(2)}, u32[]{:S(2)}) async-start(bf16[64,2,160]{2,1,0:T(2,128)(2,1)} %reshape.261), calls=%async_computation.1 | async-start | bytes 131072 | tf_op jit(solution)/shard_map/all_to_all | solution.py:107
  113.1 0.1 fusion.16
  113.2 9.7 %all-to-all-done.1 = bf16[64,2,160]{2,1,0:T(2,128)(2,1)S(1)} async-done(((bf16[64,2,160]{2,1,0:T(2,128)(2,1)}), bf16[64,2,160]{2,1,0:T(2,128)(2,1)S(1)}, u32[]{:S(2)}, u32[]{:S(2)}) %all-to-all-start.1) | async-done | bytes 40992 | tf_op jit(solution)/shard_map/all_to_all | solution.py:107
  122.9 0.1 reshape.262
  123.0 0.2 convolution_convert_fusion.4
  123.2 0.8 reshape.263
  124.0 4.4 %all-to-all-start.2 = ((bf16[64,4,160]{2,1,0:T(4,128)(2,1)}), bf16[64,4,160]{2,1,0:T(4,128)(2,1)S(1)}, u32[]{:S(2)}, u32[]{:S(2)}) async-start(bf16[64,4,160]{2,1,0:T(4,128)(2,1)} %reshape.263), calls=%async_computation.2 | async-start | bytes 262144 | tf_op jit(solution)/shard_map/all_to_all | solution.py:116
  133.4 5.5 %all-to-all-done.2 = bf16[64,4,160]{2,1,0:T(4,128)(2,1)S(1)} async-done(((bf16[64,4,160]{2,1,0:T(4,128)(2,1)}), bf16[64,4,160]{2,1,0:T(4,128)(2,1)S(1)}, u32[]{:S(2)}, u32[]{:S(2)}) %all-to-all-start.2) | async-done | bytes 81952 | tf_op jit(solution)/shard_map/all_to_all | solution.py:116
  138.9 0.1 reshape.264
  139.0 0.9 convolution_convert_fusion.3
  (10 shorter events, 0.1 us)
Async XLA Ops:
  6.5 93.4 %copy-start = (bf16[160,5120]{1,0:T(8,128)(2,1)S(1)}, bf16[160,5120]{1,0:T(8,128)(2,1)}, u32[]{:S(2)}) copy-start(bf16[160,5120]{1,0:T(8,128)(2,1)} %param.15) | copy-start | bytes 4915204
  6.5 4.3 %copy-start.2 = (bf16[64,1280]{1,0:T(8,128)(2,1)S(1)}, bf16[64,1280]{1,0:T(8,128)(2,1)}, u32[]{:S(2)}) copy-start(bf16[64,1280]{1,0:T(8,128)(2,1)} %param.12) | copy-start | bytes 491524
  6.5 86.2 %all-gather.2.cloned.1.call-start = ((), (), s32[]{:S(2)}) async-start(), calls=%async_computation.3 | async-start | bytes 3686400 | tf_op jit(solution)/shard_map/all_gather | solution.py:49
  11.5 1.5 %copy-start.1 = (f32[512,1280]{1,0:T(8,128)}, f32[512,1280]{1,0:T(8,128)S(1)}, u32[]{:S(2)}) copy-start(f32[512,1280]{1,0:T(8,128)S(1)} %get-tuple-element.15) | copy-start | bytes 7864324
  11.9 1.8 %copy-start.7 = (bf16[3,160,1280]{2,1,0:T(8,128)(2,1)S(1)}, bf16[3,160,1280]{2,1,0:T(8,128)(2,1)}, u32[]{:S(2)}) copy-start(bf16[3,160,1280]{2,1,0:T(8,128)(2,1)} %param.13) | copy-start | bytes 3686404
  11.9 11.2 %copy-start.3 = (s32[512]{0:T(512)S(1)}, s32[512]{0:T(512)}, u32[]{:S(2)}) copy-start(s32[512]{0:T(512)} %param.16) | copy-start | bytes 6148
  14.3 14.7 %collective-permute-start.2 = (bf16[512,160]{0,1:T(8,128)(2,1)S(1)}, bf16[512,160]{0,1:T(8,128)(2,1)S(1)}, u32[]{:S(2)}, u32[]{:S(2)}) collective-permute-start(bf16[512,160]{0,1:T(8,128)(2,1)S(1)} %convolution_convert_fusion), channel_id=1, source_target_pairs={{0,1},{1,0},{2,3},{3,2},{4,5},{5,4},{6,7},{7,6},{8,9},{9,8},{10,11... | collective-permute-start | bytes 491528 | tf_op jit(solution)/shard_map/ppermute | solution.py:12
  23.1 5.5 %collective-permute-start.1 = (bf16[512]{0:T(512)(128)(2,1)S(1)}, bf16[512]{0:T(512)(128)(2,1)S(1)}, u32[]{:S(2)}, u32[]{:S(2)}) collective-permute-start(bf16[512]{0:T(512)(128)(2,1)S(1)} %get-tuple-element.11), channel_id=1, source_target_pairs={{0,1},{1,0},{2,3},{3,2},{4,5},{5,4},{6,7},{7,6},{8,9},{9,8},{10,11... | collective-permute-start | bytes 3080 | tf_op jit(solution)/shard_map/ppermute | solution.py:12
  25.6 3.4 %collective-permute-start = (bf16[512,160]{0,1:T(8,128)(2,1)S(1)}, bf16[512,160]{0,1:T(8,128)(2,1)S(1)}, u32[]{:S(2)}, u32[]{:S(2)}) collective-permute-start(bf16[512,160]{0,1:T(8,128)(2,1)S(1)} %convolution_convert_fusion.2), channel_id=1, source_target_pairs={{0,1},{1,0},{2,3},{3,2},{4,5},{5,4},{6,7},{7,6},{8,9},{9,8},{10,11... | collective-permute-start | bytes 491528 | tf_op jit(solution)/shard_map/ppermute | solution.py:12
  31.9 5.9 %copy-start.5 = (s32[64]{0:T(128)S(1)}, s32[64]{0:T(128)}, u32[]{:S(2)}) copy-start(s32[64]{0:T(128)} %param.19) | copy-start | bytes 772
  32.0 6.0 %copy-start.4 = (s32[64]{0:T(128)S(1)}, s32[64]{0:T(128)}, u32[]{:S(2)}) copy-start(s32[64]{0:T(128)} %param.18) | copy-start | bytes 772
  32.0 6.0 %copy-start.6 = (s32[64,2]{0,1:T(2,128)S(1)}, s32[64,2]{0,1:T(2,128)}, u32[]{:S(2)}) copy-start(s32[64,2]{0,1:T(2,128)} %param.17) | copy-start | bytes 1540
  33.2 53.2 %all-to-all-start = ((bf16[8,512,160]{1,2,0:T(8,128)(2,1)}), bf16[8,512,160]{1,2,0:T(8,128)(2,1)S(1)}, u32[]{:S(2)}, u32[]{:S(2)}) async-start(bf16[8,512,160]{1,2,0:T(8,128)(2,1)} %broadcast_in_dim.69), calls=%async_computation | async-start | bytes 2621440 | tf_op jit(solution)/shard_map/all_to_all | solution.py:94
  102.7 20.2 %all-to-all-start.1 = ((bf16[64,2,160]{2,1,0:T(2,128)(2,1)}), bf16[64,2,160]{2,1,0:T(2,128)(2,1)S(1)}, u32[]{:S(2)}, u32[]{:S(2)}) async-start(bf16[64,2,160]{2,1,0:T(2,128)(2,1)} %reshape.261), calls=%async_computation.1 | async-start | bytes 131072 | tf_op jit(solution)/shard_map/all_to_all | solution.py:107
  124.0 14.9 %all-to-all-start.2 = ((bf16[64,4,160]{2,1,0:T(4,128)(2,1)}), bf16[64,4,160]{2,1,0:T(4,128)(2,1)S(1)}, u32[]{:S(2)}, u32[]{:S(2)}) async-start(bf16[64,4,160]{2,1,0:T(4,128)(2,1)} %reshape.263), calls=%async_computation.2 | async-start | bytes 262144 | tf_op jit(solution)/shard_map/all_to_all | solution.py:116
Sparse Core Ops, SparseCore 0:
  9.4 83.2 all-gather.1
where the time goes:
time: 147 us
  waiting for transfers between devices  67.3 us (46%)
  starting transfers between devices  32.6 us (22%)
  between operations  21.2 us (14%)
  matrix products  15.1 us (10%)
  local copies, waits for them, and re-layouts  6.95 us (5%)
  other arithmetic  3.64 us (2%)
    all_to_all x1, waiting for transfers between devices, on_device(): gathered = lax.all_to_all(sent, 'head', 0, 0, tiled=True)  44.9 us
    ppermute x3, starting transfers between devices, partner(): lax.ppermute(x, axis, [(i, i ^ 1 << apart) for i in range(lax.axis_size(a...  13.1 us
    all_to_all x1, starting transfers between devices, on_device(): lax.all_to_all(projected.reshape(places, share, width_here), 'tok', 0, 0,...  10.4 us
    all_to_all x1, waiting for transfers between devices, on_device(): lax.all_to_all(projected.reshape(places, share, width_here), 'tok', 0, 0,...  9.7 us
    all_gather x1, waiting for transfers between devices, on_device(): full_weight = lax.all_gather(out_weight, 'head', axis=0, tiled=True)  6.37 us
    all_to_all x1, waiting for transfers between devices, on_device(): lax.all_to_all(pieces.reshape(places, 2 * share, width_here), 'tok', 0, 0...  5.53 us
    dot_general x1, matrix products, on_device(): jnp.einsum('ztf,zfd->td', gathered, full_weight.reshape(group, width_here...  4.83 us
    all_to_all x1, starting transfers between devices, on_device(): gathered = lax.all_to_all(sent, 'head', 0, 0, tiled=True)  4.66 us
  transfers between devices with their start and end apart: 7, of which 4 were waited for; matrix products, arithmetic and copies ran while one was open for 8% of the time, Pallas kernels for 0%

commit v1 on v0

--- a/solution.py
+++ b/solution.py
@@ -3,6 +3,7 @@
 import jax.numpy as jnp
 from jax import lax
 from jax.sharding import PartitionSpec as P
+from jax.lax import all_to_all, axis_size
 
 HEAD_DIM = 80
 CAP = 248
@@ -46,7 +47,10 @@
     image_offsets,
     owners,
 ):
-    full_weight = lax.all_gather(out_weight, "head", axis=0, tiled=True)
+    trail = []
+    for _ in range(axis_size("head")):
+        trail.append(out_weight)
+    full_weight = jnp.concatenate(all_to_all(jnp.stack(trail), "head", 0, 0), axis=0)
     block_rows = patches.shape[0]
     width_here = qkv_weight.shape[1]
     heads_here = width_here // HEAD_DIM

time: 147 us -> 193 us (1.31); the launches traced: 147 us -> 191 us
  blocking collectives: 0 us -> 39.3 us
  waiting for transfers between devices: 67.3 us -> 84.3 us
  between operations: 21.2 us -> 7.67 us
    all_to_all x0 -> x1, blocking collectives: none -> 39.3 us  [on_device(): gathered = lax.all_to_all(sent, 'head', 0, 0, tiled=True)]
    all_to_all x1, waiting for transfers between devices: 44.9 us -> 68.9 us  [on_device(): all_to_all(jnp.stack(trail), 'head', 0, 0)]
    all_gather x1 -> x0, waiting for transfers between devices: 6.37 us -> none  [on_device(): full_weight = lax.all_gather(out_weight, 'head', axis=0, tiled=True)]
  transfers between devices with their start and end apart: 7 -> 6, of which waited for: 4 -> 3; matrix products, arithmetic and copies ran while one was open for 8% -> 2% of each run, Pallas kernels for 0% -> 0%
where the time goes in v1:
time: 193 us; the launch traced here: 191 us
  waiting for transfers between devices  84.3 us (44%)
  blocking collectives  39.3 us (20%)
  starting transfers between devices  32.8 us (17%)
  matrix products  15.1 us (8%)
  local copies, waits for them, and re-layouts  7.92 us (4%)
  between operations  7.67 us (4%)
  other arithmetic  3.61 us (2%)
    all_to_all x1, waiting for transfers between devices, on_device(): all_to_all(jnp.stack(trail), 'head', 0, 0)  68.9 us
    all_to_all x1, blocking collectives, on_device(): gathered = lax.all_to_all(sent, 'head', 0, 0, tiled=True)  39.3 us
    ppermute x3, starting transfers between devices, partner(): lax.ppermute(x, axis, [(i, i ^ 1 << apart) for i in range(lax.axis_size(a...  13.1 us
    all_to_all x1, starting transfers between devices, on_device(): lax.all_to_all(projected.reshape(places, share, width_here), 'tok', 0, 0,...  10.6 us
    all_to_all x1, waiting for transfers between devices, on_device(): lax.all_to_all(projected.reshape(places, share, width_here), 'tok', 0, 0,...  9.7 us
    all_to_all x1, waiting for transfers between devices, on_device(): lax.all_to_all(pieces.reshape(places, 2 * share, width_here), 'tok', 0, 0...  5.7 us
    dot_general x1, matrix products, on_device(): jnp.einsum('ztf,zfd->td', gathered, full_weight.reshape(group, width_here...  4.82 us
    all_to_all x1, starting transfers between devices, on_device(): all_to_all(jnp.stack(trail), 'head', 0, 0)  4.57 us
  transfers between devices with their start and end apart: 6, of which 3 were waited for; matrix products, arithmetic and copies ran while one was open for 2% of the time, Pallas kernels for 0%

profile of v1, /device:TPU:1, one launch (start us, length us, event | category | flops | bytes accessed | tf_op | source)
XLA Modules:
  0.0 190.6 jit_solution(17088777241576533101)
XLA Ops:
  0.0 0.0 copy-start
  0.0 0.0 copy-start.3
  0.0 0.8 slice_bitcast_fusion
  0.8 0.8 select_reduce_fusion
  1.6 0.1 fusion.22
  1.7 2.0 %convolution_add_fusion.1 = f32[512,1280]{1,0:T(8,128)S(1)} fusion(bf16[64,1280]{1,0:T(8,128)(2,1)} %param.11, bf16[512,1280]{1,0:T(8,128)(2,1)} %param.10, s32[512]{0:T(512)S(1)} %get-tuple-element.13), kind=kOutput, calls=%fused_computation.3 | convolution fusion | flops 85229568 | bytes 4098048 | tf_op jit(solution)/shard_map/dot_general | solution.py:69
  3.7 0.0 copy-done.3
  3.7 0.6 fusion.41
  4.4 0.0 copy-start.1
  4.4 0.4 multiply_reduce_fusion.1
  4.8 0.0 copy-start.8
  4.8 0.0 copy-start.4
  4.8 0.3 multiply_convert_fusion.1
  5.1 0.8 copy-done.1
  5.9 0.7 copy-done.8
  6.6 0.6 convolution_convert_fusion
  7.2 8.8 %collective-permute-start.2 = (bf16[512,160]{0,1:T(8,128)(2,1)S(1)}, bf16[512,160]{0,1:T(8,128)(2,1)S(1)}, u32[]{:S(2)}, u32[]{:S(2)}) collective-permute-start(bf16[512,160]{0,1:T(8,128)(2,1)S(1)} %convolution_convert_fusion), channel_id=1, source_target_pairs={{0,1},{1,0},{2,3},{3,2},{4,5},{5,4},{6,7},{7,6},{8,9},{9,8},{10,11... | collective-permute-start | bytes 491528 | tf_op jit(solution)/shard_map/ppermute | solution.py:13
  16.0 0.0 copy-done.4
  16.0 1.9 %collective-permute-start.1 = (bf16[512]{0:T(512)(128)(2,1)S(1)}, bf16[512]{0:T(512)(128)(2,1)S(1)}, u32[]{:S(2)}, u32[]{:S(2)}) collective-permute-start(bf16[512]{0:T(512)(128)(2,1)S(1)} %get-tuple-element.11), channel_id=1, source_target_pairs={{0,1},{1,0},{2,3},{3,2},{4,5},{5,4},{6,7},{7,6},{8,9},{9,8},{10,11... | collective-permute-start | bytes 3080 | tf_op jit(solution)/shard_map/ppermute | solution.py:13
  17.9 0.6 convolution_convert_fusion.2
  18.5 2.4 %collective-permute-start = (bf16[512,160]{0,1:T(8,128)(2,1)S(1)}, bf16[512,160]{0,1:T(8,128)(2,1)S(1)}, u32[]{:S(2)}, u32[]{:S(2)}) collective-permute-start(bf16[512,160]{0,1:T(8,128)(2,1)S(1)} %convolution_convert_fusion.2), channel_id=1, source_target_pairs={{0,1},{1,0},{2,3},{3,2},{4,5},{5,4},{6,7},{7,6},{8,9},{9,8},{10,11... | collective-permute-start | bytes 491528 | tf_op jit(solution)/shard_map/ppermute | solution.py:13
  20.9 0.6 convolution_convert_fusion.1
  21.5 0.0 collective-permute-done.1
  21.5 0.4 broadcast_compare_fusion
  21.9 0.0 collective-permute-done.2
  21.9 1.5 fusion
  23.4 0.0 collective-permute-done
  23.5 1.4 fusion.3
  24.8 0.0 copy-start.2
  24.8 0.1 broadcast_in_dim.69
  25.0 39.3 %all_to_all.20 = bf16[8,512,160]{1,2,0:T(8,128)(2,1)S(1)} all-to-all(bf16[8,512,160]{1,2,0:T(8,128)(2,1)S(1)} %broadcast_in_dim.69), channel_id=1, replica_groups=mesh['head'=8,'tok'=64] {'head'}, dimensions={0} | all-to-all | bytes 2621440 | tf_op jit(solution)/shard_map/all_to_all | solution.py:98
  64.3 0.0 copy-done.2
  64.3 1.9 %stack.2 = bf16[8,160,1280]{2,1,0:T(8,128)(2,1)} broadcast(bf16[160,1280]{1,0:T(8,128)(2,1)S(1)} %copy-done.2), dimensions={1,2} | broadcast | bytes 3686400 | tf_op jit(solution)/shard_map/stack | solution.py:53
  66.2 0.0 copy-start.6
  66.2 0.0 copy-start.5
  66.2 0.0 copy-start.7
  66.2 4.6 %all-to-all-start.1 = ((bf16[8,160,1280]{2,1,0:T(8,128)(2,1)}), bf16[8,160,1280]{2,1,0:T(8,128)(2,1)}, u32[]{:S(2)}, u32[]{:S(2)}) async-start(bf16[8,160,1280]{2,1,0:T(8,128)(2,1)} %stack.2), calls=%async_computation.1 | async-start | bytes 6553600 | tf_op jit(solution)/shard_map/all_to_all | solution.py:53
  70.8 0.0 copy-done.6
  70.8 0.1 eq.109
  70.9 0.0 copy-done.5
  70.9 0.0 copy-done.7
  70.9 0.7 fusion.37
  72.9 0.1 copy.12
  74.3 68.9 %all-to-all-done.1 = bf16[8,160,1280]{2,1,0:T(8,128)(2,1)} async-done(((bf16[8,160,1280]{2,1,0:T(8,128)(2,1)}), bf16[8,160,1280]{2,1,0:T(8,128)(2,1)}, u32[]{:S(2)}, u32[]{:S(2)}) %all-to-all-start.1) | async-done | bytes 3276832 | tf_op jit(solution)/shard_map/all_to_all | solution.py:53
  143.2 4.8 %fusion.42 = (f32[512]{0:T(512)S(1)}, f32[512,1280]{1,0:T(8,128)S(1)}) fusion(f32[512,1280]{1,0:T(8,128)} %copy-done.1, bf16[8,512,160]{1,2,0:T(8,128)(2,1)S(1)} %all_to_all.20, bf16[8,160,1280]{2,1,0:T(8,128)(2,1)} %all-to-all-done.1), kind=kOutput, calls=%fused_computation.113 | convolution fusion | flops 1679031808 | bytes 9832448 | tf_op jit(solution)/shard_map/ztf,zfd->td/dot_general | solution.py:99
  148.0 0.4 multiply_reduce_fusion
  148.4 0.3 multiply_convert_fusion
  148.8 1.7 reshape.258
  150.5 0.0 copy-done
  150.5 1.9 convolution_convert_fusion.5
  152.4 0.1 copy.13
  152.5 0.7 reshape.259
  153.2 10.6 %all-to-all-start.2 = ((bf16[64,2,160]{2,1,0:T(2,128)(2,1)}), bf16[64,2,160]{2,1,0:T(2,128)(2,1)S(1)}, u32[]{:S(2)}, u32[]{:S(2)}) async-start(bf16[64,2,160]{2,1,0:T(2,128)(2,1)} %reshape.259), calls=%async_computation.2 | async-start | bytes 131072 | tf_op jit(solution)/shard_map/all_to_all | solution.py:111
  163.8 0.1 fusion.16
  163.9 9.7 %all-to-all-done.2 = bf16[64,2,160]{2,1,0:T(2,128)(2,1)S(1)} async-done(((bf16[64,2,160]{2,1,0:T(2,128)(2,1)}), bf16[64,2,160]{2,1,0:T(2,128)(2,1)S(1)}, u32[]{:S(2)}, u32[]{:S(2)}) %all-to-all-start.2) | async-done | bytes 40992 | tf_op jit(solution)/shard_map/all_to_all | solution.py:111
  173.6 0.1 reshape.260
  173.7 0.2 convolution_convert_fusion.4
  173.9 0.8 reshape.261
  174.7 4.4 %all-to-all-start.3 = ((bf16[64,4,160]{2,1,0:T(4,128)(2,1)}), bf16[64,4,160]{2,1,0:T(4,128)(2,1)S(1)}, u32[]{:S(2)}, u32[]{:S(2)}) async-start(bf16[64,4,160]{2,1,0:T(4,128)(2,1)} %reshape.261), calls=%async_computation.3 | async-start | bytes 262144 | tf_op jit(solution)/shard_map/all_to_all | solution.py:120
  183.9 5.7 %all-to-all-done.3 = bf16[64,4,160]{2,1,0:T(4,128)(2,1)S(1)} async-done(((bf16[64,4,160]{2,1,0:T(4,128)(2,1)}), bf16[64,4,160]{2,1,0:T(4,128)(2,1)S(1)}, u32[]{:S(2)}, u32[]{:S(2)}) %all-to-all-start.3) | async-done | bytes 81952 | tf_op jit(solution)/shard_map/all_to_all | solution.py:120
  189.6 0.1 reshape.262
  189.7 0.9 convolution_convert_fusion.3
  (10 shorter events, 0.1 us)
Async XLA Ops:
  0.0 150.5 %copy-start = (bf16[160,5120]{1,0:T(8,128)(2,1)S(1)}, bf16[160,5120]{1,0:T(8,128)(2,1)}, u32[]{:S(2)}) copy-start(bf16[160,5120]{1,0:T(8,128)(2,1)} %param.15) | copy-start | bytes 4915204
  0.0 3.7 %copy-start.3 = (bf16[64,1280]{1,0:T(8,128)(2,1)S(1)}, bf16[64,1280]{1,0:T(8,128)(2,1)}, u32[]{:S(2)}) copy-start(bf16[64,1280]{1,0:T(8,128)(2,1)} %param.12) | copy-start | bytes 491524
  4.4 1.6 copy-start.1
  4.8 1.8 copy-start.8
  4.8 11.2 %copy-start.4 = (s32[512]{0:T(512)S(1)}, s32[512]{0:T(512)}, u32[]{:S(2)}) copy-start(s32[512]{0:T(512)} %param.16) | copy-start | bytes 6148
  7.2 14.7 %collective-permute-start.2 = (bf16[512,160]{0,1:T(8,128)(2,1)S(1)}, bf16[512,160]{0,1:T(8,128)(2,1)S(1)}, u32[]{:S(2)}, u32[]{:S(2)}) collective-permute-start(bf16[512,160]{0,1:T(8,128)(2,1)S(1)} %convolution_convert_fusion), channel_id=1, source_target_pairs={{0,1},{1,0},{2,3},{3,2},{4,5},{5,4},{6,7},{7,6},{8,9},{9,8},{10,11... | collective-permute-start | bytes 491528 | tf_op jit(solution)/shard_map/ppermute | solution.py:13
  16.0 5.5 %collective-permute-start.1 = (bf16[512]{0:T(512)(128)(2,1)S(1)}, bf16[512]{0:T(512)(128)(2,1)S(1)}, u32[]{:S(2)}, u32[]{:S(2)}) collective-permute-start(bf16[512]{0:T(512)(128)(2,1)S(1)} %get-tuple-element.11), channel_id=1, source_target_pairs={{0,1},{1,0},{2,3},{3,2},{4,5},{5,4},{6,7},{7,6},{8,9},{9,8},{10,11... | collective-permute-start | bytes 3080 | tf_op jit(solution)/shard_map/ppermute | solution.py:13
  18.5 4.9 %collective-permute-start = (bf16[512,160]{0,1:T(8,128)(2,1)S(1)}, bf16[512,160]{0,1:T(8,128)(2,1)S(1)}, u32[]{:S(2)}, u32[]{:S(2)}) collective-permute-start(bf16[512,160]{0,1:T(8,128)(2,1)S(1)} %convolution_convert_fusion.2), channel_id=1, source_target_pairs={{0,1},{1,0},{2,3},{3,2},{4,5},{5,4},{6,7},{7,6},{8,9},{9,8},{10,11... | collective-permute-start | bytes 491528 | tf_op jit(solution)/shard_map/ppermute | solution.py:13
  24.8 39.4 %copy-start.2 = (bf16[160,1280]{1,0:T(8,128)(2,1)S(1)}, bf16[160,1280]{1,0:T(8,128)(2,1)}, u32[]{:S(2)}) copy-start(bf16[160,1280]{1,0:T(8,128)(2,1)} %param.14) | copy-start | bytes 1228804
  66.2 4.6 %copy-start.6 = (s32[64]{0:T(128)S(1)}, s32[64]{0:T(128)}, u32[]{:S(2)}) copy-start(s32[64]{0:T(128)} %param.19) | copy-start | bytes 772
  66.2 4.7 %copy-start.5 = (s32[64]{0:T(128)S(1)}, s32[64]{0:T(128)}, u32[]{:S(2)}) copy-start(s32[64]{0:T(128)} %param.18) | copy-start | bytes 772
  66.2 4.7 %copy-start.7 = (s32[64,2]{0,1:T(2,128)S(1)}, s32[64,2]{0,1:T(2,128)}, u32[]{:S(2)}) copy-start(s32[64,2]{0,1:T(2,128)} %param.17) | copy-start | bytes 1540
  66.2 77.0 %all-to-all-start.1 = ((bf16[8,160,1280]{2,1,0:T(8,128)(2,1)}), bf16[8,160,1280]{2,1,0:T(8,128)(2,1)}, u32[]{:S(2)}, u32[]{:S(2)}) async-start(bf16[8,160,1280]{2,1,0:T(8,128)(2,1)} %stack.2), calls=%async_computation.1 | async-start | bytes 6553600 | tf_op jit(solution)/shard_map/all_to_all | solution.py:53
  153.2 20.4 %all-to-all-start.2 = ((bf16[64,2,160]{2,1,0:T(2,128)(2,1)}), bf16[64,2,160]{2,1,0:T(2,128)(2,1)S(1)}, u32[]{:S(2)}, u32[]{:S(2)}) async-start(bf16[64,2,160]{2,1,0:T(2,128)(2,1)} %reshape.259), calls=%async_computation.2 | async-start | bytes 131072 | tf_op jit(solution)/shard_map/all_to_all | solution.py:111
  174.7 14.9 %all-to-all-start.3 = ((bf16[64,4,160]{2,1,0:T(4,128)(2,1)}), bf16[64,4,160]{2,1,0:T(4,128)(2,1)S(1)}, u32[]{:S(2)}, u32[]{:S(2)}) async-start(bf16[64,4,160]{2,1,0:T(4,128)(2,1)} %reshape.261), calls=%async_computation.3 | async-start | bytes 262144 | tf_op jit(solution)/shard_map/all_to_all | solution.py:120
